TPU v7x, 32 devices: a whole 2x2x4 slice. The times are simulated.
32 devices in a mesh: dp: 4 (over y, x), wide: 8 (over z, core).
Axes of the slice: x: 2, y: 2, z: 4, core: 2. Of those that a mesh axis runs over, the one named last changes fastest.
Arguments:
- clips: bfloat16 [4, 8, 4, 128, 512], P('dp', 'wide'), may hold values from -8 to 8
- w_spatial: bfloat16 [4608, 512], P(None, 'dp'), may hold values from -0.09375 to 0.09375
- w_time: bfloat16 [1536, 512], replicated, may hold values from -0.15625 to 0.15625
- norm_gain: float32 [512], replicated, may hold values from 0.1 to 1.9
- norm_bias: float32 [512], replicated, may hold values from -0.6 to 0.6
- grad_out: bfloat16 [4, 8, 512, 512], P('dp', None, 'wide'), may hold values from -6 to 6
Outputs:
- grad_clips: bfloat16 [4, 8, 4, 128, 512], P('dp', 'wide')
- spatial_grad: float32 [4608, 512], P('dp', 'wide')
- time_grad: float32 [1536, 512], P('dp', 'wide')
All inputs are finite; a program needn't handle non-finite values.
Results may differ from a plain program's by a relative error of at most 0.009.
Values may be sent and summed in bfloat16 or wider, within the bound.
No kernel may reach another device: no remote copies, remote signals or barrier semaphores. Data moves between devices by JAX's collectives and lax.ppermute only.
A program may use at most 128 MiB of HBM per device.

v0:
```python
import jax
import jax.numpy as jnp
from jax import lax
from jax.sharding import PartitionSpec as P

G = 32
FRAMES = 8
EPSILON = 1e-06
CONTRACT_ROWS = (((0,), (0,)), ((), ()))
CONTRACT_COLS = (((1,), (1,)), ((), ()))


def pad_frames(frames):
    return jnp.pad(frames, ((0, 0), (1, 1), (1, 1), (0, 0)))


def spatial_forward(frames, weights):
    frame_total, row_count, col_count, chan_count = frames.shape
    padded = pad_frames(frames)
    accum_out = jnp.zeros((frame_total * row_count * col_count, weights.shape[1]), jnp.float32)
    for tap_index in range(9):
        row_off, col_off = (tap_index // 3, tap_index % 3)
        window = padded[:, row_off : row_off + row_count, col_off : col_off + col_count, :].reshape(
            -1, chan_count
        )
        tap_weight = weights[tap_index * chan_count : (tap_index + 1) * chan_count]
        accum_out = accum_out + jnp.dot(window, tap_weight, preferred_element_type=jnp.float32)
    return accum_out.reshape(frame_total, row_count, col_count, -1)


def spatial_backward(frames, grad_hidden, weights):
    frame_total, row_count, col_count, chan_count = frames.shape
    padded_in = pad_frames(frames)
    padded_grad = pad_frames(grad_hidden)
    grad_flat = grad_hidden.reshape(-1, chan_count)
    grad_input = jnp.zeros((frame_total * row_count * col_count, chan_count), jnp.float32)
    tap_grads = []
    for tap_index in range(9):
        row_off, col_off = (tap_index // 3, tap_index % 3)
        window = padded_in[
            :, row_off : row_off + row_count, col_off : col_off + col_count, :
        ].reshape(-1, chan_count)
        tap_grads.append(
            lax.dot_general(window, grad_flat, CONTRACT_ROWS, preferred_element_type=jnp.float32)
        )
        flipped = padded_grad[
            :, 2 - row_off : 2 - row_off + row_count, 2 - col_off : 2 - col_off + col_count, :
        ].reshape(-1, chan_count)
        tap_weight = weights[tap_index * chan_count : (tap_index + 1) * chan_count]
        grad_input = grad_input + lax.dot_general(
            flipped, tap_weight, CONTRACT_COLS, preferred_element_type=jnp.float32
        )
    return (grad_input.reshape(frames.shape), jnp.concatenate(tap_grads, axis=0))


def norm_forward(hidden, norm_gain, norm_bias):
    frame_total, row_count, col_count, chan_count = hidden.shape
    grouped = hidden.astype(jnp.float32).reshape(
        frame_total, row_count * col_count, G, chan_count // G
    )
    group_mean = jnp.mean(grouped, axis=(1, 3), keepdims=True)
    centered = grouped - group_mean
    variance = jnp.mean(centered * centered, axis=(1, 3), keepdims=True)
    inv_std = lax.rsqrt(variance + EPSILON)
    normed = centered * inv_std
    preact = normed.reshape(hidden.shape) * norm_gain + norm_bias
    return (preact, normed, inv_std)


def norm_backward(grad_act, preact, normed, inv_std, norm_gain):
    sigmoid_z = jax.nn.sigmoid(preact)
    grad_pre = grad_act.astype(jnp.float32) * sigmoid_z * (1.0 + preact * (1.0 - sigmoid_z))
    grad_normed = (grad_pre * norm_gain).reshape(normed.shape)
    mean_grad = jnp.mean(grad_normed, axis=(1, 3), keepdims=True)
    mean_proj = jnp.mean(grad_normed * normed, axis=(1, 3), keepdims=True)
    return ((grad_normed - mean_grad - normed * mean_proj) * inv_std).reshape(preact.shape)


def temporal_backward(tiles, grad_out, w_time):
    clip_count, frame_total, pix_count, chan_count = tiles.shape
    grad_act = jnp.zeros(tiles.shape, jnp.float32)
    tap_grads = []
    for tap_index in range(3):
        kept = frame_total - tap_index
        earlier = tiles[:, :kept].reshape(-1, chan_count)
        later = grad_out[:, tap_index:].reshape(-1, chan_count)
        tap_grads.append(
            lax.dot_general(earlier, later, CONTRACT_ROWS, preferred_element_type=jnp.float32)
        )
        tap_weight = w_time[tap_index * chan_count : (tap_index + 1) * chan_count]
        back_part = lax.dot_general(
            later, tap_weight, CONTRACT_COLS, preferred_element_type=jnp.float32
        )
        back_part = back_part.reshape(clip_count, kept, pix_count, chan_count)
        grad_act = grad_act + jnp.pad(back_part, ((0, 0), (0, tap_index), (0, 0), (0, 0)))
    return (jnp.concatenate(tap_grads, axis=0), grad_act)


def shards(clips, w_spatial, w_time, norm_gain, norm_bias, grad_out):
    group_count, frame_count, row_count, col_count, chan_count = clips.shape
    frames = clips.reshape(group_count * frame_count, row_count, col_count, chan_count)
    weights = lax.all_gather(w_spatial, "dp", axis=1, tiled=True)
    hidden = spatial_forward(frames, weights).astype(jnp.bfloat16)
    preact, normed, inv_std = norm_forward(hidden, norm_gain, norm_bias)
    act = (
        jax.nn.silu(preact)
        .astype(jnp.bfloat16)
        .reshape(group_count, frame_count, row_count * col_count, chan_count)
    )
    tiles = lax.all_to_all(act, "wide", split_axis=2, concat_axis=1, tiled=True)
    tile_shape = tiles.shape
    by_clip = tiles.reshape(-1, FRAMES, tile_shape[2], tile_shape[3])
    grad_clipwise = grad_out.reshape(by_clip.shape)
    time_raw, grad_act = temporal_backward(by_clip, grad_clipwise, w_time)
    grad_act = grad_act.astype(jnp.bfloat16).reshape(tile_shape)
    returned = lax.all_to_all(grad_act, "wide", split_axis=1, concat_axis=2, tiled=True)
    grad_hidden = norm_backward(
        returned.reshape(frames.shape), preact, normed, inv_std, norm_gain
    ).astype(jnp.bfloat16)
    grad_input, spatial_raw = spatial_backward(frames, grad_hidden, weights)
    position_total = (
        group_count
        * frame_count
        * row_count
        * col_count
        * lax.axis_size("wide")
        * lax.axis_size("dp")
    )
    grad_scale = float(position_total) ** (-0.5)
    partial_pair = (
        lax.psum_scatter(spatial_raw, "wide", scatter_dimension=1, tiled=True),
        lax.psum_scatter(time_raw, "wide", scatter_dimension=1, tiled=True),
    )
    spatial_sum, time_sum = (
        lax.psum_scatter(partial_pair[0], "dp", scatter_dimension=0, tiled=True),
        lax.psum_scatter(partial_pair[1], "dp", scatter_dimension=0, tiled=True),
    )
    grad_clips = grad_input.astype(jnp.bfloat16).reshape(clips.shape)
    return (grad_clips, spatial_sum * grad_scale, time_sum * grad_scale)


def solution(mesh):
    return jax.shard_map(
        shards,
        mesh=mesh,
        in_specs=(
            P("dp", "wide", None, None, None),
            P(None, "dp"),
            P(),
            P(),
            P(),
            P("dp", None, "wide", None),
        ),
        out_specs=(P("dp", "wide", None, None, None), P("dp", "wide"), P("dp", "wide")),
        check_vma=False,
    )
```

profile of v0, /device:TPU:0, one launch (start us, length us, event | category | flops | bytes accessed | tf_op | source)
XLA Modules:
  0.0 337.8 jit_solution(4861131859740784181)
XLA Ops:
  11.1 2.3 fusion.15
  13.4 6.4 %all-to-all-start = ((bf16[1,8,64,512]{3,2,0,1:T(8,128)(2,1)}), bf16[1,8,64,512]{3,2,0,1:T(8,128)(2,1)S(1)}, u32[]{:S(2)}, u32[]{:S(2)}) async-start(bf16[1,8,64,512]{3,2,0,1:T(8,128)(2,1)} %fusion.15), calls=%async_computation | async-start | bytes 1048576 | tf_op jit(solution)/shard_map/all_to_all | solution.py:116
  20.1 2.5 pad_slice_fusion
  22.6 2.1 copy.46
  24.7 2.0 copy.40
  26.7 2.1 copy.41
  28.8 2.0 copy.42
  30.8 2.0 copy.43
  32.9 2.0 copy.44
  36.9 32.4 %all-gather.2.cloned.1.call-done = bf16[4608,512]{1,0:T(8,128)(2,1)} async-done(((bf16[4608,128]{1,0:T(8,128)(2,1)}), bf16[4608,512]{1,0:T(8,128)(2,1)}) %all-gather.2.cloned.1.call-update) | async-done | bytes 4718608 | tf_op jit(solution)/shard_map/all_gather | solution.py:102
  82.4 5.6 %reduce.16 = bf16[512,512]{1,0:T(8,128)(2,1)} reduce(bf16[512,1,1,512]{3,2,1,0:T(2,128)(2,1)} %bitcast.222, bf16[]{:T(256)} %broadcast.543), dimensions={1,2}, to_apply=%bitcast.194.reduce_sub_computation | reduce | bytes 1048578
  88.0 2.2 reshape.596
  90.2 20.0 %all_to_all.21 = bf16[8,2,16384]{2,1,0:T(2,128)(2,1)} all-to-all(bf16[8,2,16384]{2,1,0:T(2,128)(2,1)} %reshape.596), channel_id=1, replica_groups=mesh['dp'=4,'wide'=8] {'wide'}, dimensions={0} | all-to-all | bytes 1048576 | tf_op jit(solution)/shard_map/all_to_all | solution.py:110
  110.2 3.5 %reshape.597 = bf16[512,1,1,512]{3,2,1,0:T(2,128)(2,1)} reshape(bf16[8,2,16384]{2,1,0:T(2,128)(2,1)} %all_to_all.21) | data formatting | bytes 1048576
  116.4 2.0 pad_maximum_fusion
  118.4 3.6 %copy.53 = f32[1536,512]{0,1:T(8,128)} copy(f32[1536,512]{1,0:T(8,128)} %pad_maximum_fusion) | data formatting | bytes 6291456
  136.8 9.7 %copy.51 = f32[4608,512]{0,1:T(8,128)} copy(f32[4608,512]{1,0:T(8,128)} %fusion) | data formatting | bytes 18874368
  146.6 13.9 %reduce-scatter.15.cloned.1.call-done = f32[64,1536]{1,0:T(8,128)} async-done(((f32[512,1536]{1,0:T(8,128)}), f32[64,1536]{1,0:T(8,128)}) %reduce-scatter.15.cloned.1.call-update) | async-done | bytes 393232
  160.5 2.2 copy.54
  163.4 1.9 pad_slice_fusion.8
  166.8 94.7 %reduce-scatter.13.cloned.1.call-done = f32[64,4608]{1,0:T(8,128)} async-done(((f32[512,4608]{1,0:T(8,128)}), f32[64,4608]{1,0:T(8,128)}) %reduce-scatter.13.cloned.1.call-update) | async-done | bytes 1179664
  261.5 2.9 copy.52
  273.1 15.9 %reduce-scatter.11.cloned.1.call-done = f32[384,64]{1,0:T(8,128)} async-done(((f32[1536,64]{1,0:T(8,128)}), f32[384,64]{1,0:T(8,128)}) %reduce-scatter.11.cloned.1.call-update) | async-done | bytes 98320 | tf_op jit(solution)/shard_map/reduce_scatter | solution.py:136
  290.6 38.6 %reduce-scatter.9.cloned.1.call-done = f32[1152,64]{1,0:T(8,128)} async-done(((f32[4608,64]{1,0:T(8,128)}), f32[1152,64]{1,0:T(8,128)}) %reduce-scatter.9.cloned.1.call-update) | async-done | bytes 294928 | tf_op jit(solution)/shard_map/reduce_scatter | solution.py:135
  (115 shorter events, 51.1 us)
Async XLA Ops:
  7.2 3.9 %copy-start.1 = (bf16[1,8,64,512]{3,2,1,0:T(8,128)(2,1)S(1)}, bf16[1,8,64,512]{3,2,1,0:T(8,128)(2,1)}, u32[]{:S(2)}) copy-start(bf16[1,8,64,512]{3,2,1,0:T(8,128)(2,1)} %param.11) | copy-start | bytes 1572868
  7.2 12.6 %copy-start.2 = (bf16[1,1,4,128,512]{4,3,2,1,0:T(8,128)(2,1)S(1)}, bf16[1,1,4,128,512]{4,3,2,1,0:T(8,128)(2,1)}, u32[]{:S(2)}) copy-start(bf16[1,1,4,128,512]{4,3,2,1,0:T(8,128)(2,1)} %param.6) | copy-start | bytes 1572868
  7.2 62.2 %all-gather.2.cloned.1.call-start = ((), (), s32[]{:S(2)}) async-start(), calls=%async_computation.6 | async-start | bytes 5898240 | tf_op jit(solution)/shard_map/all_gather | solution.py:102
  13.4 63.6 %all-to-all-start = ((bf16[1,8,64,512]{3,2,0,1:T(8,128)(2,1)}), bf16[1,8,64,512]{3,2,0,1:T(8,128)(2,1)S(1)}, u32[]{:S(2)}, u32[]{:S(2)}) async-start(bf16[1,8,64,512]{3,2,0,1:T(8,128)(2,1)} %fusion.15), calls=%async_computation | async-start | bytes 1048576 | tf_op jit(solution)/shard_map/all_to_all | solution.py:116
  19.8 140.7 %reduce-scatter.15.cloned.1.call-start = ((), (), s32[]{:S(2)}) async-start(), calls=%async_computation.10 | async-start | bytes 3538944
  35.9 37.4 %copy-start.12 = (bf16[1,4,128,512]{3,2,1,0:T(8,128)(2,1)S(1)}, bf16[1,4,128,512]{3,2,1,0:T(8,128)(2,1)}, u32[]{:S(2)}) copy-start(bf16[1,4,128,512]{3,2,1,0:T(8,128)(2,1)} %copy.42) | copy-start | bytes 1572868
  36.9 35.9 %copy-start.13 = (bf16[1,4,128,512]{3,2,1,0:T(8,128)(2,1)S(1)}, bf16[1,4,128,512]{3,2,1,0:T(8,128)(2,1)}, u32[]{:S(2)}) copy-start(bf16[1,4,128,512]{3,2,1,0:T(8,128)(2,1)} %copy.41) | copy-start | bytes 1572868
  69.4 3.4 %copy-start = (bf16[4608,512]{1,0:T(8,128)(2,1)S(1)}, bf16[4608,512]{1,0:T(8,128)(2,1)}, u32[]{:S(2)}) copy-start(bf16[4608,512]{1,0:T(8,128)(2,1)} %all-gather.2.cloned.1.call-done) | copy-start | bytes 14155780
  72.8 1.4 copy-start.11
  73.3 1.4 copy-start.10
  73.7 1.4 copy-start.9
  74.2 1.4 copy-start.8
  74.7 2.3 copy-start.14
  74.7 2.3 copy-start.15
  122.0 139.5 %reduce-scatter.13.cloned.1.call-start = ((), (), s32[]{:S(2)}) async-start(), calls=%async_computation.9 | async-start | bytes 10616832
  123.5 5.9 %copy-start.3 = (bf16[1,1,4,128,512]{4,3,2,1,0:T(8,128)(2,1)S(1)}, bf16[1,1,4,128,512]{4,3,2,1,0:T(8,128)(2,1)}, u32[]{:S(2)}) copy-start(bf16[1,1,4,128,512]{4,3,2,1,0:T(8,128)(2,1)} %param.6) | copy-start | bytes 1572868
  146.5 142.4 %reduce-scatter.11.cloned.1.call-start = ((), (), s32[]{:S(2)}) async-start(), calls=%async_computation.8 | async-start | bytes 983040 | tf_op jit(solution)/shard_map/reduce_scatter | solution.py:136
  162.7 166.6 %reduce-scatter.9.cloned.1.call-start = ((), (), s32[]{:S(2)}) async-start(), calls=%async_computation.7 | async-start | bytes 2949120 | tf_op jit(solution)/shard_map/reduce_scatter | solution.py:135
  261.5 8.3 %slice-start = ((s8[4718592]{0:T(1024)(128)(4,1)}), s8[524288]{0:T(1024)(128)(4,1)S(1)}, s32[]{:S(2)}) async-start(s8[4718592]{0:T(1024)(128)(4,1)} %bitcast.214), calls=%async_computation.11 | async-start | bytes 1048576
  264.5 5.3 %slice-start.1 = ((s8[4718592]{0:T(1024)(128)(4,1)}), s8[4194304]{0:T(1024)(128)(4,1)S(1)}, s32[]{:S(2)}) async-start(s8[4718592]{0:T(1024)(128)(4,1)} %bitcast.214), calls=%async_computation.12 | async-start | bytes 8388608
  266.3 4.0 %copy-start.7 = (bf16[1,4,128,512]{3,2,1,0:T(8,128)(2,1)S(1)}, bf16[1,4,128,512]{3,2,1,0:T(8,128)(2,1)}, u32[]{:S(2)}) copy-start(bf16[1,4,128,512]{3,2,1,0:T(8,128)(2,1)} %get-tuple-element.24) | copy-start | bytes 1572868
  268.0 2.8 copy-start.6
  269.8 1.5 copy-start.5
  270.3 1.5 copy-start.4
Sparse Core Ops, SparseCore 0:
  9.8 59.5 all-gather.1
  122.1 38.3 reduce-scatter.14
  162.8 98.6 reduce-scatter.12
  264.3 24.6 reduce-scatter.10
  291.8 37.3 reduce-scatter.8
where the time goes:
time: 339 us; the launch traced here: 338 us
  waiting for transfers between devices  196 us (58%)
  local copies, waits for them, and re-layouts  49.4 us (15%)
  matrix products  36.5 us (11%)
  blocking collectives  20 us (6%)
  other arithmetic  14.8 us (4%)
  between operations  14.3 us (4%)
  starting transfers between devices  6.55 us (2%)
    unnamed x7, waiting for transfers between devices  109 us
    reduce_scatter x1, waiting for transfers between devices, shards(): lax.psum_scatter(partial_pair[0], 'dp', scatter_dimension=0, tiled=True)  38.6 us
    all_gather x1, waiting for transfers between devices, shards(): weights = lax.all_gather(w_spatial, 'dp', axis=1, tiled=True)  32.4 us
    unnamed x47, local copies, waits for them, and re-layouts  27.9 us
    all_to_all x1, blocking collectives, shards(): tiles = lax.all_to_all(act, 'wide', split_axis=2, concat_axis=1, tiled=True)  20 us
    slice x9, local copies, waits for them, and re-layouts, spatial_forward(): padded[:, row_off:row_off + row_count, col_off:col_off + col_count, :]  16.8 us
    reduce_scatter x1, waiting for transfers between devices, shards(): lax.psum_scatter(partial_pair[1], 'dp', scatter_dimension=0, tiled=True)  15.9 us
    dot_general x9, matrix products, spatial_backward(): lax.dot_general(window, grad_flat, CONTRACT_ROWS, preferred_element_type=...  13.3 us
  transfers between devices with their start and end apart: 6, of which 5 were waited for; matrix products, arithmetic and copies ran while one was open for 22% of the time, Pallas kernels for 0%

commit v1 on v0

--- a/solution.py
+++ b/solution.py
@@ -107,7 +107,13 @@
         .astype(jnp.bfloat16)
         .reshape(group_count, frame_count, row_count * col_count, chan_count)
     )
-    tiles = lax.all_to_all(act, "wide", split_axis=2, concat_axis=1, tiled=True)
+    low = jax.lax.all_to_all(
+        jnp.stack(jnp.split(act, jax.lax.axis_size("wide"), axis=2), 0),
+        split_axis=0,
+        concat_axis=0,
+        axis_name="wide",
+    )
+    tiles = jnp.concatenate(low, 1)
     tile_shape = tiles.shape
     by_clip = tiles.reshape(-1, FRAMES, tile_shape[2], tile_shape[3])
     grad_clipwise = grad_out.reshape(by_clip.shape)

time: 339 us -> 324 us (0.956)
  local copies, waits for them, and re-layouts: 49.4 us -> 40.2 us
  other arithmetic: 14.8 us -> 9.23 us
    unnamed x47 -> x50, local copies, waits for them, and re-layouts: 27.9 us -> 20.4 us
    unnamed x2 -> x1, other arithmetic: 5.56 us -> 0.01 us
  transfers between devices with their start and end apart: 6 -> 6, of which waited for: 5 -> 5; matrix products, arithmetic and copies ran while one was open for 22% -> 23% of each run, Pallas kernels for 0% -> 0%
where the time goes in v1:
time: 324 us; the launch traced here: 323 us
  waiting for transfers between devices  196 us (60%)
  local copies, waits for them, and re-layouts  40.2 us (12%)
  matrix products  36.6 us (11%)
  blocking collectives  19.7 us (6%)
  between operations  14.3 us (4%)
  other arithmetic  9.23 us (3%)
  starting transfers between devices  6.73 us (2%)
    unnamed x7, waiting for transfers between devices  109 us
    reduce_scatter x1, waiting for transfers between devices, shards(): lax.psum_scatter(partial_pair[0], 'dp', scatter_dimension=0, tiled=True)  38.6 us
    all_gather x1, waiting for transfers between devices, shards(): weights = lax.all_gather(w_spatial, 'dp', axis=1, tiled=True)  32.4 us
    unnamed x50, local copies, waits for them, and re-layouts  20.4 us
    all_to_all x1, blocking collectives, shards(): jax.lax.all_to_all(jnp.stack(jnp.split(act, jax.lax.axis_size('wide'), ax...  19.7 us
    slice x9, local copies, waits for them, and re-layouts, spatial_forward(): padded[:, row_off:row_off + row_count, col_off:col_off + col_count, :]  16.9 us
    reduce_scatter x1, waiting for transfers between devices, shards(): lax.psum_scatter(partial_pair[1], 'dp', scatter_dimension=0, tiled=True)  15.9 us
    dot_general x9, matrix products, spatial_backward(): lax.dot_general(window, grad_flat, CONTRACT_ROWS, preferred_element_type=...  13.3 us
  transfers between devices with their start and end apart: 6, of which 5 were waited for; matrix products, arithmetic and copies ran while one was open for 23% of the time, Pallas kernels for 0%

profile of v1, /device:TPU:0, one launch (start us, length us, event | category | flops | bytes accessed | tf_op | source)
XLA Modules:
  0.0 322.8 jit_solution(10546165293153323364)
XLA Ops:
  11.1 2.3 fusion.15
  13.4 6.4 %all-to-all-start = ((bf16[1,8,64,512]{3,2,0,1:T(8,128)(2,1)}), bf16[1,8,64,512]{3,2,0,1:T(8,128)(2,1)S(1)}, u32[]{:S(2)}, u32[]{:S(2)}) async-start(bf16[1,8,64,512]{3,2,0,1:T(8,128)(2,1)} %fusion.15), calls=%async_computation | async-start | bytes 1048576 | tf_op jit(solution)/shard_map/all_to_all | solution.py:122
  20.1 2.5 pad_slice_fusion
  22.7 2.1 copy.32
  24.7 2.0 copy.26
  26.8 2.1 copy.27
  28.8 2.0 copy.28
  30.9 2.0 copy.29
  32.9 2.1 copy.30
  37.0 32.4 %all-gather.2.cloned.1.call-done = bf16[4608,512]{1,0:T(8,128)(2,1)} async-done(((bf16[4608,128]{1,0:T(8,128)(2,1)}), bf16[4608,512]{1,0:T(8,128)(2,1)}) %all-gather.2.cloned.1.call-update) | async-done | bytes 4718608 | tf_op jit(solution)/shard_map/all_gather | solution.py:102
  69.4 1.8 fusion.56
  80.2 19.7 %all_to_all.14 = bf16[8,1,1,64,512]{4,3,2,1,0:T(8,128)(2,1)S(1)} all-to-all(bf16[8,1,1,64,512]{4,3,2,1,0:T(8,128)(2,1)S(1)} %fusion.66), channel_id=1, replica_groups=mesh['dp'=4,'wide'=8] {'wide'}, dimensions={0} | all-to-all | bytes 1048576 | tf_op jit(solution)/shard_map/all_to_all | solution.py:110
  101.4 2.0 pad_maximum_fusion
  103.3 3.6 %copy.38 = f32[1536,512]{0,1:T(8,128)} copy(f32[1536,512]{1,0:T(8,128)} %pad_maximum_fusion) | data formatting | bytes 6291456
  122.0 9.7 %copy.36 = f32[4608,512]{0,1:T(8,128)} copy(f32[4608,512]{1,0:T(8,128)} %fusion) | data formatting | bytes 18874368
  131.7 13.7 %reduce-scatter.15.cloned.1.call-done = f32[64,1536]{1,0:T(8,128)} async-done(((f32[512,1536]{1,0:T(8,128)}), f32[64,1536]{1,0:T(8,128)}) %reduce-scatter.15.cloned.1.call-update) | async-done | bytes 393232
  145.4 2.2 copy.39
  148.4 1.9 pad_slice_fusion.8
  151.8 94.7 %reduce-scatter.13.cloned.1.call-done = f32[64,4608]{1,0:T(8,128)} async-done(((f32[512,4608]{1,0:T(8,128)}), f32[64,4608]{1,0:T(8,128)}) %reduce-scatter.13.cloned.1.call-update) | async-done | bytes 1179664
  246.6 2.9 copy.37
  249.5 1.8 convolution_add_fusion.7
  253.1 1.7 convolution_add_fusion.5
  258.1 15.9 %reduce-scatter.11.cloned.1.call-done = f32[384,64]{1,0:T(8,128)} async-done(((f32[1536,64]{1,0:T(8,128)}), f32[384,64]{1,0:T(8,128)}) %reduce-scatter.11.cloned.1.call-update) | async-done | bytes 98320 | tf_op jit(solution)/shard_map/reduce_scatter | solution.py:142
  275.7 38.6 %reduce-scatter.9.cloned.1.call-done = f32[1152,64]{1,0:T(8,128)} async-done(((f32[4608,64]{1,0:T(8,128)}), f32[1152,64]{1,0:T(8,128)}) %reduce-scatter.9.cloned.1.call-update) | async-done | bytes 294928 | tf_op jit(solution)/shard_map/reduce_scatter | solution.py:141
  (117 shorter events, 42.4 us)
Async XLA Ops:
  7.2 3.9 %copy-start.1 = (bf16[1,8,64,512]{3,2,1,0:T(8,128)(2,1)S(1)}, bf16[1,8,64,512]{3,2,1,0:T(8,128)(2,1)}, u32[]{:S(2)}) copy-start(bf16[1,8,64,512]{3,2,1,0:T(8,128)(2,1)} %param.11) | copy-start | bytes 1572868
  7.2 12.7 %copy-start.2 = (bf16[1,1,4,128,512]{4,3,2,1,0:T(8,128)(2,1)S(1)}, bf16[1,1,4,128,512]{4,3,2,1,0:T(8,128)(2,1)}, u32[]{:S(2)}) copy-start(bf16[1,1,4,128,512]{4,3,2,1,0:T(8,128)(2,1)} %param.6) | copy-start | bytes 1572868
  7.2 62.2 %all-gather.2.cloned.1.call-start = ((), (), s32[]{:S(2)}) async-start(), calls=%async_computation.6 | async-start | bytes 5898240 | tf_op jit(solution)/shard_map/all_gather | solution.py:102
  13.4 63.6 %all-to-all-start = ((bf16[1,8,64,512]{3,2,0,1:T(8,128)(2,1)}), bf16[1,8,64,512]{3,2,0,1:T(8,128)(2,1)S(1)}, u32[]{:S(2)}, u32[]{:S(2)}) async-start(bf16[1,8,64,512]{3,2,0,1:T(8,128)(2,1)} %fusion.15), calls=%async_computation | async-start | bytes 1048576 | tf_op jit(solution)/shard_map/all_to_all | solution.py:122
  19.8 125.7 %reduce-scatter.15.cloned.1.call-start = ((), (), s32[]{:S(2)}) async-start(), calls=%async_computation.10 | async-start | bytes 3538944
  36.0 37.3 %copy-start.12 = (bf16[1,4,128,512]{3,2,1,0:T(8,128)(2,1)S(1)}, bf16[1,4,128,512]{3,2,1,0:T(8,128)(2,1)}, u32[]{:S(2)}) copy-start(bf16[1,4,128,512]{3,2,1,0:T(8,128)(2,1)} %copy.28) | copy-start | bytes 1572868
  37.0 35.8 %copy-start.13 = (bf16[1,4,128,512]{3,2,1,0:T(8,128)(2,1)S(1)}, bf16[1,4,128,512]{3,2,1,0:T(8,128)(2,1)}, u32[]{:S(2)}) copy-start(bf16[1,4,128,512]{3,2,1,0:T(8,128)(2,1)} %copy.27) | copy-start | bytes 1572868
  69.4 3.4 %copy-start = (bf16[4608,512]{1,0:T(8,128)(2,1)S(1)}, bf16[4608,512]{1,0:T(8,128)(2,1)}, u32[]{:S(2)}) copy-start(bf16[4608,512]{1,0:T(8,128)(2,1)} %all-gather.2.cloned.1.call-done) | copy-start | bytes 14155780
  72.8 1.4 copy-start.11
  73.3 1.4 copy-start.10
  73.7 1.4 copy-start.9
  74.2 1.4 copy-start.8
  74.7 2.3 copy-start.14
  74.7 2.3 copy-start.15
  107.0 139.6 %reduce-scatter.13.cloned.1.call-start = ((), (), s32[]{:S(2)}) async-start(), calls=%async_computation.9 | async-start | bytes 10616832
  108.7 5.9 %copy-start.3 = (bf16[1,1,4,128,512]{4,3,2,1,0:T(8,128)(2,1)S(1)}, bf16[1,1,4,128,512]{4,3,2,1,0:T(8,128)(2,1)}, u32[]{:S(2)}) copy-start(bf16[1,1,4,128,512]{4,3,2,1,0:T(8,128)(2,1)} %param.6) | copy-start | bytes 1572868
  131.7 142.3 %reduce-scatter.11.cloned.1.call-start = ((), (), s32[]{:S(2)}) async-start(), calls=%async_computation.8 | async-start | bytes 983040 | tf_op jit(solution)/shard_map/reduce_scatter | solution.py:142
  147.6 166.6 %reduce-scatter.9.cloned.1.call-start = ((), (), s32[]{:S(2)}) async-start(), calls=%async_computation.7 | async-start | bytes 2949120 | tf_op jit(solution)/shard_map/reduce_scatter | solution.py:141
  246.5 8.3 %slice-start = ((s8[4718592]{0:T(1024)(128)(4,1)}), s8[524288]{0:T(1024)(128)(4,1)S(1)}, s32[]{:S(2)}) async-start(s8[4718592]{0:T(1024)(128)(4,1)} %bitcast.241), calls=%async_computation.11 | async-start | bytes 1048576
  249.5 5.3 %slice-start.1 = ((s8[4718592]{0:T(1024)(128)(4,1)}), s8[4194304]{0:T(1024)(128)(4,1)S(1)}, s32[]{:S(2)}) async-start(s8[4718592]{0:T(1024)(128)(4,1)} %bitcast.241), calls=%async_computation.12 | async-start | bytes 8388608
  251.3 4.0 %copy-start.7 = (bf16[1,4,128,512]{3,2,1,0:T(8,128)(2,1)S(1)}, bf16[1,4,128,512]{3,2,1,0:T(8,128)(2,1)}, u32[]{:S(2)}) copy-start(bf16[1,4,128,512]{3,2,1,0:T(8,128)(2,1)} %get-tuple-element.21) | copy-start | bytes 1572868
  253.1 2.8 copy-start.6
  254.8 1.5 copy-start.5
  255.3 1.5 copy-start.4
Sparse Core Ops, SparseCore 0:
  9.8 59.5 all-gather.1
  107.1 38.3 reduce-scatter.14
  147.7 98.7 reduce-scatter.12
  249.3 24.6 reduce-scatter.10
  276.9 37.3 reduce-scatter.8
